TPU v7x, 128 devices: a whole 4x4x4 slice. The times are simulated.
128 devices in a mesh: row: 4 (over x), col: 32 (over y, z, core).
Axes of the slice: x: 4, y: 4, z: 4, core: 2. Of those that a mesh axis runs over, the one named last changes fastest.
Arguments:
- ancestor_inverse: float32 [16384, 16384], P('col', 'row'), as said below
- panels: float32 [2, 16384, 512], P(None, ('col', 'row')), may hold values from -0.1875 to 0.1875
- pattern: int32 [2, 128, 2], replicated, may hold values 0 or 1
- diag_inverse: float32 [2, 512, 512], replicated, may hold values from -6 to 6
- link_panel: float32 [512, 512], replicated, may hold values from -0.25 to 0.25
- block_list: int32 [32, 4, 32], P('col', 'row'), may hold values from 0 to 7
- gauge_owner: int32 [32, 4, 32], P('col', 'row'), may hold values from 0 to 31, each once within a row
- gauge_weight: float32 [4, 32, 512], P('row', 'col'), may hold values from -0.25 to 0.25
Outputs:
- y_first: float32 [16384, 512], P(('col', 'row'))
- diag_first: float32 [512, 512], replicated
- y_second: float32 [16384, 512], P(('col', 'row'))
- cross_second: float32 [512, 512], replicated
- diag_second: float32 [512, 512], replicated
- gauge_response: float32 [4, 32, 512], P('row', 'col')
Inputs may be any that keep to these rules, and one draw needn't show every extreme that they name: `ancestor_inverse`: with its columns put in natural order the matrix is symmetric.
All inputs are finite; a program needn't handle non-finite values.
Results may differ from a plain program's by a relative error of at most 0.000092.
Values sent between devices are 32-bit elements; how exact they have to be, the bound alone decides.
No kernel may reach another device: no remote copies, remote signals or barrier semaphores. Data moves between devices by JAX's collectives and lax.ppermute only.
A program may use at most 128 MiB of HBM per device.

v0:
```python
import jax
import jax.numpy as jnp
from jax import lax
from jax.sharding import Mesh, PartitionSpec as P

NIB = 8
IBR = 16
HIGH = lax.Precision.HIGH
COL = ("y", "z", "core")
CHIPS = ("x", "y", "z")


def dot(left, right, left_dim=1, right_dim=0, precision=HIGH):
    return lax.dot_general(
        left,
        right,
        (((left_dim,), (right_dim,)), ((), ())),
        precision=precision,
        preferred_element_type=jnp.float32,
    )


def swap_core(value):
    return lax.ppermute(value, "core", [(0, 1), (1, 0)])


def spread(value, axes, count):
    copies = jnp.broadcast_to(value[None], (count,) + value.shape)
    return lax.all_to_all(copies, axes, 0, 0, tiled=True)


def all_sum(partial):
    rows, width = partial.shape
    core = lax.axis_index("core")
    halves = partial.reshape(2, rows // 2, width)
    mine = lax.dynamic_index_in_dim(halves, core, 0, keepdims=False)
    theirs = lax.dynamic_index_in_dim(halves, 1 - core, 0, keepdims=False)
    half = mine + swap_core(theirs)
    pieces = half.reshape(64, rows // 128, width)
    part = lax.all_to_all(pieces, CHIPS, 0, 0, tiled=True).sum(0)
    whole = spread(part, CHIPS, 64).reshape(rows // 2, width)
    other = swap_core(whole)
    first = core == 0
    return jnp.concatenate([jnp.where(first, whole, other), jnp.where(first, other, whole)], 0)


def local(ancestor, panels, pattern, diag_inverse, link, block_list, gauge_owner, gauge_weight):
    row = lax.axis_index("x")
    col = lax.axis_index("y") * 8 + lax.axis_index("z") * 2 + lax.axis_index("core")
    flags = lax.dynamic_index_in_dim(pattern, col * 4 + row, 1, keepdims=False)
    flags = jnp.repeat(flags.astype(jnp.float32), 256, axis=1)
    masked = panels * flags[:, None, :]
    both = jnp.concatenate([masked[0], masked[1]], axis=1)
    gathered = lax.all_gather(both, COL, axis=0, tiled=True)
    own_rows = spread(both, "x", 4).reshape(512, 1024)
    weights = lax.all_to_all(gauge_weight.reshape(32, IBR), COL, 0, 0, tiled=True)
    owner_match = (gauge_owner[0, 0][None, :] == jnp.arange(32, dtype=jnp.int32)[:, None]).astype(
        jnp.float32
    )
    block_match = (block_list[0, 0][:, None] == jnp.arange(NIB, dtype=jnp.int32)[None, :]).astype(
        jnp.float32
    )
    selector = dot(owner_match, block_match, precision=lax.Precision.HIGHEST)
    combine = (selector[:, :, None] * weights[:, None, :]).reshape(32, NIB * IBR)
    z = dot(ancestor, gathered)
    g_first = dot(own_rows[:, :512], z[:, :512], 0, 0)
    g_cross = dot(z[:, :512], own_rows[:, 512:], 0, 0)
    g_second = dot(own_rows[:, 512:], z[:, 512:], 0, 0)
    z_rows = lax.all_to_all(z.reshape(4, 128, 1024), "x", 0, 0, tiled=True).sum(0)
    grams = all_sum(jnp.concatenate([g_first, g_cross, g_second], 0))
    y_first = -z_rows[:, :512]
    y_second = -(z_rows[:, 512:] + dot(y_first, link))
    shares = dot(combine, y_second)
    gauge = lax.all_to_all(shares, COL, 0, 0, tiled=True).sum(0).reshape(1, 1, 512)
    diag_first = diag_inverse[0] + grams[:512]
    cross = grams[512:1024]
    cross_second = cross - dot(diag_first, link)
    diag_second = (
        diag_inverse[1] + grams[1024:] - dot(cross, link, 0, 0) - dot(link, cross_second, 0, 0)
    )
    return (y_first, diag_first, y_second, cross_second, diag_second, gauge)


def solution(mesh):
    grid = Mesh(mesh.devices.reshape(4, 4, 4, 2), ("x", "y", "z", "core"))
    in_specs = (
        P(COL, "x"),
        P(None, COL + ("x",), None),
        P(),
        P(),
        P(),
        P(COL, "x", None),
        P(COL, "x", None),
        P("x", COL, None),
    )
    out_specs = (P(COL + ("x",), None), P(), P(COL + ("x",), None), P(), P(), P("x", COL, None))
    return jax.shard_map(local, mesh=grid, in_specs=in_specs, out_specs=out_specs, check_vma=False)
```

profile of v0, /device:TPU:1, one launch (start us, length us, event | category | flops | bytes accessed | tf_op | source)
XLA Modules:
  0.0 265.8 jit_solution(2948248204228471022)
XLA Ops:
  7.2 0.9 convert_reduce_fusion
  8.2 1.1 broadcast_multiply_fusion
  9.4 0.8 pad_maximum_fusion.2
  10.2 2.6 broadcast_in_dim.7
  12.9 4.8 %all-to-all-start.1 = ((f32[4,128,1024]{2,1,0:T(8,128)}), f32[4,128,1024]{2,1,0:T(8,128)S(1)}, u32[]{:S(2)}, u32[]{:S(2)}) async-start(f32[4,128,1024]{2,1,0:T(8,128)} %broadcast_in_dim.7), calls=%async_computation.1 | async-start | bytes 4194304 | tf_op jit(solution)/shard_map/all_to_all | solution.py:29
  17.7 69.4 %all-gather.2.cloned.1.call-done = f32[4096,1024]{1,0:T(8,128)} async-done(((f32[128,1024]{1,0:T(8,128)}), f32[4096,1024]{1,0:T(8,128)}) %all-gather.2.cloned.1.call-update) | async-done | bytes 16777232 | tf_op jit(solution)/shard_map/all_gather | solution.py:54
  87.1 19.4 %fusion.16 = f32[1024,512]{0,1:T(8,128)} fusion(f32[4096,1024]{1,0:T(8,128)} %all-gather.2.cloned.1.call-done, f32[512,4096]{1,0:T(8,128)} %param.8), kind=kOutput, calls=%fused_computation.38 | convolution fusion | flops 12884901888 | bytes 27262976 | tf_op jit(solution)/shard_map/dot_general | solution.py:14
  106.5 2.3 fusion.3
  108.8 2.3 fusion.8
  111.1 2.3 fusion.5
  113.6 1.6 copy-done.1
  115.9 3.3 %collective-permute-done = f32[768,512]{1,0:T(8,128)} collective-permute-done((f32[768,512]{1,0:T(8,128)S(1)}, f32[768,512]{1,0:T(8,128)}, u32[]{:S(2)}, u32[]{:S(2)}) %collective-permute-start) | collective-permute-done | bytes 1572896 | tf_op jit(solution)/shard_map/ppermute | solution.py:24
  119.2 2.2 bitcast_add_fusion
  121.4 1.5 reshape.52
  122.9 8.3 %all-to-all-start.2 = ((f32[64,12,512]{2,1,0:T(8,128)}), f32[64,12,512]{2,1,0:T(8,128)S(1)}, u32[]{:S(2)}, u32[]{:S(2)}) async-start(f32[64,12,512]{2,1,0:T(8,128)} %reshape.52), calls=%async_computation.2 | async-start | bytes 4194304 | tf_op jit(solution)/shard_map/all_to_all | solution.py:40
  133.1 25.8 %all-to-all-done.2 = f32[64,12,512]{2,1,0:T(8,128)S(1)} async-done(((f32[64,12,512]{2,1,0:T(8,128)}), f32[64,12,512]{2,1,0:T(8,128)S(1)}, u32[]{:S(2)}, u32[]{:S(2)}) %all-to-all-start.2) | async-done | bytes 1572896 | tf_op jit(solution)/shard_map/all_to_all | solution.py:40
  158.9 6.5 %all-to-all-start.4 = ((f32[32,1,16]{2,1,0:T(1,128)}), f32[32,1,16]{2,1,0:T(1,128)S(1)}, u32[]{:S(2)}, u32[]{:S(2)}) async-start(f32[32,1,16]{2,1,0:T(1,128)} %bitcast.13), calls=%async_computation.4 | async-start | bytes 32768 | tf_op jit(solution)/shard_map/all_to_all | solution.py:56
  165.5 6.8 %all-to-all-done.4 = f32[32,1,16]{2,1,0:T(1,128)S(1)} async-done(((f32[32,1,16]{2,1,0:T(1,128)}), f32[32,1,16]{2,1,0:T(1,128)S(1)}, u32[]{:S(2)}, u32[]{:S(2)}) %all-to-all-start.4) | async-done | bytes 2080 | tf_op jit(solution)/shard_map/all_to_all | solution.py:56
  172.6 32.3 %all_to_all.38 = f32[64,12,512]{2,1,0:T(8,128)S(1)} all-to-all(f32[64,12,512]{2,1,0:T(8,128)S(1)} %broadcast_in_dim.8), channel_id=1, replica_groups=mesh['x'=4,'y'=4,'z'=4,'core'=2] {'x','y','z'}, dimensions={0} | all-to-all | bytes 3145728 | tf_op jit(solution)/shard_map/all_to_all | solution.py:29
  204.9 4.4 %all-to-all-start = ((f32[4,128,1024]{2,1,0:T(8,128)}), f32[4,128,1024]{2,1,0:T(8,128)}, u32[]{:S(2)}, u32[]{:S(2)}) async-start(f32[4,128,1024]{2,1,0:T(8,128)} %bitcast.3), calls=%async_computation | async-start | bytes 4194304 | tf_op jit(solution)/shard_map/all_to_all | solution.py:69
  209.3 1.3 reshape.53
  210.7 2.9 %collective-permute-start.1 = (f32[768,512]{1,0:T(8,128)}, f32[768,512]{1,0:T(8,128)}, u32[]{:S(2)}, u32[]{:S(2)}) collective-permute-start(f32[768,512]{1,0:T(8,128)} %reshape.53), channel_id=1, source_target_pairs={{0,1},{1,0},{2,3},{3,2},{4,5},{5,4},{6,7},{7,6},{8,9},{9,8},{10,11... | collective-permute-start | bytes 4718600 | tf_op jit(solution)/shard_map/ppermute | solution.py:24
  213.9 19.0 %all-to-all-done = f32[4,128,1024]{2,1,0:T(8,128)} async-done(((f32[4,128,1024]{2,1,0:T(8,128)}), f32[4,128,1024]{2,1,0:T(8,128)}, u32[]{:S(2)}, u32[]{:S(2)}) %all-to-all-start) | async-done | bytes 2097184 | tf_op jit(solution)/shard_map/all_to_all | solution.py:69
  232.9 1.8 reduce_sum.27
  235.2 0.7 copy-done.7
  236.1 0.7 copy.21
  236.8 7.6 %all-to-all-start.5 = ((f32[32,1,512]{2,1,0:T(1,128)}), f32[32,1,512]{2,1,0:T(1,128)S(1)}, u32[]{:S(2)}, u32[]{:S(2)}) async-start(f32[32,1,512]{2,1,0:T(1,128)} %copy.21), calls=%async_computation.5 | async-start | bytes 131072 | tf_op jit(solution)/shard_map/all_to_all | solution.py:74
  244.4 7.4 %all-to-all-done.5 = f32[32,1,512]{2,1,0:T(1,128)S(1)} async-done(((f32[32,1,512]{2,1,0:T(1,128)}), f32[32,1,512]{2,1,0:T(1,128)S(1)}, u32[]{:S(2)}, u32[]{:S(2)}) %all-to-all-start.5) | async-done | bytes 65568 | tf_op jit(solution)/shard_map/all_to_all | solution.py:74
  252.5 1.9 broadcast_select_fusion
  254.7 1.0 convolution_subtract_fusion
  255.8 1.0 convolution_bitcast_fusion
  256.8 2.2 fusion.2
  (43 shorter events, 5.4 us)
Async XLA Ops:
  7.2 227.5 %copy-start = (f32[512,512]{1,0:T(8,128)S(1)}, f32[512,512]{1,0:T(8,128)}, u32[]{:S(2)}) copy-start(f32[512,512]{1,0:T(8,128)} %param.12) | copy-start | bytes 3145732
  7.2 79.9 %all-gather.2.cloned.1.call-start = ((), (), s32[]{:S(2)}) async-start(), calls=%async_computation.6 | async-start | bytes 17301504 | tf_op jit(solution)/shard_map/all_gather | solution.py:54
  12.9 93.7 %all-to-all-start.1 = ((f32[4,128,1024]{2,1,0:T(8,128)}), f32[4,128,1024]{2,1,0:T(8,128)S(1)}, u32[]{:S(2)}, u32[]{:S(2)}) async-start(f32[4,128,1024]{2,1,0:T(8,128)} %broadcast_in_dim.7), calls=%async_computation.1 | async-start | bytes 4194304 | tf_op jit(solution)/shard_map/all_to_all | solution.py:29
  113.6 1.6 copy-start.1
  115.4 3.8 %collective-permute-start = (f32[768,512]{1,0:T(8,128)S(1)}, f32[768,512]{1,0:T(8,128)}, u32[]{:S(2)}, u32[]{:S(2)}) collective-permute-start(f32[768,512]{1,0:T(8,128)S(1)} %dynamic-slice_bitcast_fusion), channel_id=1, source_target_pairs={{0,1},{1,0},{2,3},{3,2},{4,5},{5,4},{6,7},{7,6},{8,9},{9,8},{10,11... | collective-permute-start | bytes 4718600 | tf_op jit(solution)/shard_map/ppermute | solution.py:24
  122.9 8.8 %copy-start.8 = (f32[1,1,512]{2,1,0:T(1,128)S(1)}, f32[1,1,512]{2,1,0:T(1,128)}, u32[]{:S(2)}) copy-start(f32[1,1,512]{2,1,0:T(1,128)} %param.15) | copy-start | bytes 6148
  122.9 35.9 %all-to-all-start.2 = ((f32[64,12,512]{2,1,0:T(8,128)}), f32[64,12,512]{2,1,0:T(8,128)S(1)}, u32[]{:S(2)}, u32[]{:S(2)}) async-start(f32[64,12,512]{2,1,0:T(8,128)} %reshape.52), calls=%async_computation.2 | async-start | bytes 4194304 | tf_op jit(solution)/shard_map/all_to_all | solution.py:40
  158.9 13.4 %all-to-all-start.4 = ((f32[32,1,16]{2,1,0:T(1,128)}), f32[32,1,16]{2,1,0:T(1,128)S(1)}, u32[]{:S(2)}, u32[]{:S(2)}) async-start(f32[32,1,16]{2,1,0:T(1,128)} %bitcast.13), calls=%async_computation.4 | async-start | bytes 32768 | tf_op jit(solution)/shard_map/all_to_all | solution.py:56
  204.9 28.0 %all-to-all-start = ((f32[4,128,1024]{2,1,0:T(8,128)}), f32[4,128,1024]{2,1,0:T(8,128)}, u32[]{:S(2)}, u32[]{:S(2)}) async-start(f32[4,128,1024]{2,1,0:T(8,128)} %bitcast.3), calls=%async_computation | async-start | bytes 4194304 | tf_op jit(solution)/shard_map/all_to_all | solution.py:69
  209.3 4.3 %copy-start.9 = (s32[1,1,32]{2,1,0:T(1,128)S(1)}, s32[1,1,32]{2,1,0:T(1,128)}, u32[]{:S(2)}) copy-start(s32[1,1,32]{2,1,0:T(1,128)} %param.13) | copy-start | bytes 388
  209.3 4.2 %copy-start.10 = (s32[1,1,32]{2,1,0:T(1,128)S(1)}, s32[1,1,32]{2,1,0:T(1,128)}, u32[]{:S(2)}) copy-start(s32[1,1,32]{2,1,0:T(1,128)} %param.14) | copy-start | bytes 388
  210.7 41.8 %collective-permute-start.1 = (f32[768,512]{1,0:T(8,128)}, f32[768,512]{1,0:T(8,128)}, u32[]{:S(2)}, u32[]{:S(2)}) collective-permute-start(f32[768,512]{1,0:T(8,128)} %reshape.53), channel_id=1, source_target_pairs={{0,1},{1,0},{2,3},{3,2},{4,5},{5,4},{6,7},{7,6},{8,9},{9,8},{10,11... | collective-permute-start | bytes 4718600 | tf_op jit(solution)/shard_map/ppermute | solution.py:24
  234.7 17.8 %copy-start.2 = (f32[768,512]{1,0:T(8,128)S(1)}, f32[768,512]{1,0:T(8,128)}, u32[]{:S(2)}) copy-start(f32[768,512]{1,0:T(8,128)} %reshape.53) | copy-start | bytes 4718596
  234.7 19.7 %copy-start.6 = (f32[128,512]{1,0:T(8,128)}, f32[128,512]{1,0:T(8,128)S(1)}, u32[]{:S(2)}) copy-start(f32[128,512]{1,0:T(8,128)S(1)} %slice_negate_fusion) | copy-start | bytes 786436
  235.2 0.7 copy-start.7
  236.8 15.0 %all-to-all-start.5 = ((f32[32,1,512]{2,1,0:T(1,128)}), f32[32,1,512]{2,1,0:T(1,128)S(1)}, u32[]{:S(2)}, u32[]{:S(2)}) async-start(f32[32,1,512]{2,1,0:T(1,128)} %copy.21), calls=%async_computation.5 | async-start | bytes 131072 | tf_op jit(solution)/shard_map/all_to_all | solution.py:74
  252.5 2.1 copy-start.5
  254.7 1.0 copy-start.3
  255.8 3.2 %copy-start.4 = (f32[512,512]{1,0:T(8,128)}, f32[512,512]{1,0:T(8,128)S(1)}, u32[]{:S(2)}) copy-start(f32[512,512]{1,0:T(8,128)S(1)} %convolution_subtract_fusion) | copy-start | bytes 3145732
Sparse Core Ops, SparseCore 0:
  10.9 76.2 all-gather.1
where the time goes:
time: 267 us; the launch traced here: 266 us
  waiting for transfers between devices  132 us (49%)
  starting transfers between devices  35.1 us (13%)
  blocking collectives  32.3 us (12%)
  matrix products  31.3 us (12%)
  between operations  14.3 us (5%)
  other arithmetic  10.8 us (4%)
  local copies, waits for them, and re-layouts  10.4 us (4%)
    all_gather x1, waiting for transfers between devices, local(): gathered = lax.all_gather(both, COL, axis=0, tiled=True)  69.4 us
    all_to_all x1, blocking collectives, spread(): return lax.all_to_all(copies, axes, 0, 0, tiled=True)  32.3 us
    dot_general x10, matrix products, dot(): lax.dot_general(left, right, (((left_dim,), (right_dim,)), ((), ())), pre...  31.3 us
    all_to_all x1, waiting for transfers between devices, all_sum(): part = lax.all_to_all(pieces, CHIPS, 0, 0, tiled=True).sum(0)  25.8 us
    all_to_all x1, waiting for transfers between devices, local(): lax.all_to_all(z.reshape(4, 128, 1024), 'x', 0, 0, tiled=True).sum(0)  19 us
    all_to_all x1, starting transfers between devices, all_sum(): part = lax.all_to_all(pieces, CHIPS, 0, 0, tiled=True).sum(0)  8.28 us
    all_to_all x1, starting transfers between devices, local(): lax.all_to_all(shares, COL, 0, 0, tiled=True).sum(0).reshape(1, 1, 512)  7.64 us
    all_to_all x1, waiting for transfers between devices, local(): lax.all_to_all(shares, COL, 0, 0, tiled=True).sum(0).reshape(1, 1, 512)  7.36 us
  transfers between devices with their start and end apart: 8, of which 6 were waited for; matrix products, arithmetic and copies ran while one was open for 11% of the time, Pallas kernels for 0%

commit v1 on v0

--- a/solution.py
+++ b/solution.py
@@ -1,3 +1,4 @@
+import functools
 import jax
 import jax.numpy as jnp
 from jax import lax
@@ -8,6 +9,21 @@
 HIGH = lax.Precision.HIGH
 COL = ("y", "z", "core")
 CHIPS = ("x", "y", "z")
+
+
+def _drive_task(z_in, which_axis):
+    return jnp.concatenate(
+        lax.all_to_all(
+            jnp.stack([z_in for _ in range(lax.psum(1, which_axis))]),
+            which_axis,
+            split_axis=0,
+            concat_axis=0,
+        ),
+        axis=0,
+    )
+
+
+store_columns = functools.partial(_drive_task, which_axis=COL)
 
 
 def dot(left, right, left_dim=1, right_dim=0, precision=HIGH):
@@ -51,7 +67,7 @@
     flags = jnp.repeat(flags.astype(jnp.float32), 256, axis=1)
     masked = panels * flags[:, None, :]
     both = jnp.concatenate([masked[0], masked[1]], axis=1)
-    gathered = lax.all_gather(both, COL, axis=0, tiled=True)
+    gathered = store_columns(both)
     own_rows = spread(both, "x", 4).reshape(512, 1024)
     weights = lax.all_to_all(gauge_weight.reshape(32, IBR), COL, 0, 0, tiled=True)
     owner_match = (gauge_owner[0, 0][None, :] == jnp.arange(32, dtype=jnp.int32)[:, None]).astype(

time: 267 us -> 474 us (1.78)
  waiting for transfers between devices: 132 us -> 293 us
  starting transfers between devices: 35.1 us -> 88 us
  between operations: 14.3 us -> 0.93 us
  local copies, waits for them, and re-layouts: 10.4 us -> 17.3 us
    all_to_all x0 -> x1, waiting for transfers between devices: none -> 231 us  [_drive_task(): lax.all_to_all(jnp.stack([z_in for _ in range(lax.psum(1, which_axis))]),...]
    all_gather x1 -> x0, waiting for transfers between devices: 69.4 us -> none  [local(): gathered = lax.all_gather(both, COL, axis=0, tiled=True)]
    all_to_all x1, starting transfers between devices: 8.28 us -> 42.4 us  [all_sum(): part = lax.all_to_all(pieces, CHIPS, 0, 0, tiled=True).sum(0)]
    ppermute x2, starting transfers between devices: 3.38 us -> 13.3 us  [swap_core(): return lax.ppermute(value, 'core', [(0, 1), (1, 0)])]
    all_to_all x0 -> x1, starting transfers between devices: none -> 9.66 us  [_drive_task(): lax.all_to_all(jnp.stack([z_in for _ in range(lax.psum(1, which_axis))]),...]
    another operation x0 -> x1, local copies, waits for them, and re-layouts: none -> 7.9 us  [_drive_task(): jnp.stack([z_in for _ in range(lax.psum(1, which_axis))])]
  transfers between devices with their start and end apart: 8 -> 8, of which waited for: 6 -> 6; matrix products, arithmetic and copies ran while one was open for 11% -> 6% of each run, Pallas kernels for 0% -> 0%
where the time goes in v1:
time: 474 us; the launch traced here: 473 us
  waiting for transfers between devices  293 us (62%)
  starting transfers between devices  88 us (19%)
  blocking collectives  32.3 us (7%)
  matrix products  31.3 us (7%)
  local copies, waits for them, and re-layouts  17.3 us (4%)
  other arithmetic  10 us (2%)
    all_to_all x1, waiting for transfers between devices, _drive_task(): lax.all_to_all(jnp.stack([z_in for _ in range(lax.psum(1, which_axis))]),...  231 us
    all_to_all x1, starting transfers between devices, all_sum(): part = lax.all_to_all(pieces, CHIPS, 0, 0, tiled=True).sum(0)  42.4 us
    all_to_all x1, blocking collectives, spread(): return lax.all_to_all(copies, axes, 0, 0, tiled=True)  32.3 us
    dot_general x10, matrix products, dot(): lax.dot_general(left, right, (((left_dim,), (right_dim,)), ((), ())), pre...  31.3 us
    all_to_all x1, waiting for transfers between devices, all_sum(): part = lax.all_to_all(pieces, CHIPS, 0, 0, tiled=True).sum(0)  25.7 us
    all_to_all x1, waiting for transfers between devices, local(): lax.all_to_all(z.reshape(4, 128, 1024), 'x', 0, 0, tiled=True).sum(0)  19 us
    ppermute x2, starting transfers between devices, swap_core(): return lax.ppermute(value, 'core', [(0, 1), (1, 0)])  13.3 us
    all_to_all x1, starting transfers between devices, _drive_task(): lax.all_to_all(jnp.stack([z_in for _ in range(lax.psum(1, which_axis))]),...  9.66 us
  transfers between devices with their start and end apart: 8, of which 6 were waited for; matrix products, arithmetic and copies ran while one was open for 6% of the time, Pallas kernels for 0%

profile of v1, /device:TPU:1, one launch (start us, length us, event | category | flops | bytes accessed | tf_op | source)
XLA Modules:
  0.0 473.0 jit_solution(3849887678184761845)
XLA Ops:
  0.7 0.9 convert_reduce_fusion
  1.7 1.1 broadcast_multiply_fusion
  2.9 7.9 %stack.2 = f32[32,128,1024]{2,1,0:T(8,128)} broadcast(f32[128,1024]{1,0:T(8,128)S(1)} %pad_maximum_fusion.2), dimensions={1,2} | broadcast | bytes 17301504 | tf_op jit(solution)/shard_map/stack | solution.py:17
  10.8 9.7 %all-to-all-start = ((f32[32,128,1024]{2,1,0:T(8,128)}), f32[32,128,1024]{2,1,0:T(8,128)}, u32[]{:S(2)}, u32[]{:S(2)}) async-start(f32[32,128,1024]{2,1,0:T(8,128)} %stack.2), calls=%async_computation | async-start | bytes 33554432 | tf_op jit(solution)/shard_map/all_to_all | solution.py:16
  20.4 231.2 %all-to-all-done = f32[32,128,1024]{2,1,0:T(8,128)} async-done(((f32[32,128,1024]{2,1,0:T(8,128)}), f32[32,128,1024]{2,1,0:T(8,128)}, u32[]{:S(2)}, u32[]{:S(2)}) %all-to-all-start) | async-done | bytes 16777248 | tf_op jit(solution)/shard_map/all_to_all | solution.py:16
  251.6 1.6 broadcast_in_dim.7
  253.2 4.0 all-to-all-start.2
  257.2 19.4 %fusion.16 = f32[1024,512]{0,1:T(8,128)} fusion(f32[4096,1024]{1,0:T(8,128)} %bitcast.2, f32[512,4096]{1,0:T(8,128)} %param.8), kind=kOutput, calls=%fused_computation.38 | convolution fusion | flops 12884901888 | bytes 27262976 | tf_op jit(solution)/shard_map/dot_general | solution.py:30
  276.6 2.2 fusion.5
  278.9 2.3 fusion.8
  281.1 2.3 fusion.3
  283.7 1.6 copy-done.1
  285.5 10.4 %collective-permute-start = (f32[768,512]{1,0:T(8,128)S(1)}, f32[768,512]{1,0:T(8,128)}, u32[]{:S(2)}, u32[]{:S(2)}) collective-permute-start(f32[768,512]{1,0:T(8,128)S(1)} %dynamic-slice_bitcast_fusion), channel_id=1, source_target_pairs={{0,1},{1,0},{2,3},{3,2},{4,5},{5,4},{6,7},{7,6},{8,9},{9,8},{10,11... | collective-permute-start | bytes 4718600 | tf_op jit(solution)/shard_map/ppermute | solution.py:40
  295.9 3.2 collective-permute-done
  299.0 2.2 bitcast_add_fusion
  301.3 1.5 reshape.58
  302.8 42.4 %all-to-all-start.3 = ((f32[64,12,512]{2,1,0:T(8,128)}), f32[64,12,512]{2,1,0:T(8,128)S(1)}, u32[]{:S(2)}, u32[]{:S(2)}) async-start(f32[64,12,512]{2,1,0:T(8,128)} %reshape.58), calls=%async_computation.3 | async-start | bytes 4194304 | tf_op jit(solution)/shard_map/all_to_all | solution.py:56
  347.1 25.7 %all-to-all-done.3 = f32[64,12,512]{2,1,0:T(8,128)S(1)} async-done(((f32[64,12,512]{2,1,0:T(8,128)}), f32[64,12,512]{2,1,0:T(8,128)S(1)}, u32[]{:S(2)}, u32[]{:S(2)}) %all-to-all-start.3) | async-done | bytes 1572896 | tf_op jit(solution)/shard_map/all_to_all | solution.py:56
  372.8 6.5 %all-to-all-start.5 = ((f32[32,1,16]{2,1,0:T(1,128)}), f32[32,1,16]{2,1,0:T(1,128)S(1)}, u32[]{:S(2)}, u32[]{:S(2)}) async-start(f32[32,1,16]{2,1,0:T(1,128)} %bitcast.14), calls=%async_computation.5 | async-start | bytes 32768 | tf_op jit(solution)/shard_map/all_to_all | solution.py:72
  379.5 6.8 %all-to-all-done.5 = f32[32,1,16]{2,1,0:T(1,128)S(1)} async-done(((f32[32,1,16]{2,1,0:T(1,128)}), f32[32,1,16]{2,1,0:T(1,128)S(1)}, u32[]{:S(2)}, u32[]{:S(2)}) %all-to-all-start.5) | async-done | bytes 2080 | tf_op jit(solution)/shard_map/all_to_all | solution.py:72
  386.5 32.3 %all_to_all.43 = f32[64,12,512]{2,1,0:T(8,128)S(1)} all-to-all(f32[64,12,512]{2,1,0:T(8,128)S(1)} %broadcast_in_dim.8), channel_id=1, replica_groups=mesh['x'=4,'y'=4,'z'=4,'core'=2] {'x','y','z'}, dimensions={0} | all-to-all | bytes 3145728 | tf_op jit(solution)/shard_map/all_to_all | solution.py:45
  418.9 4.5 all-to-all-start.1
  423.3 1.3 reshape.59
  424.7 2.9 collective-permute-start.1
  427.9 19.0 %all-to-all-done.1 = f32[4,128,1024]{2,1,0:T(8,128)} async-done(((f32[4,128,1024]{2,1,0:T(8,128)}), f32[4,128,1024]{2,1,0:T(8,128)}, u32[]{:S(2)}, u32[]{:S(2)}) %all-to-all-start.1) | async-done | bytes 2097184 | tf_op jit(solution)/shard_map/all_to_all | solution.py:85
  446.9 1.8 reduce_sum.27
  450.8 7.6 %all-to-all-start.6 = ((f32[32,1,512]{2,1,0:T(1,128)}), f32[32,1,512]{2,1,0:T(1,128)S(1)}, u32[]{:S(2)}, u32[]{:S(2)}) async-start(f32[32,1,512]{2,1,0:T(1,128)} %copy.21), calls=%async_computation.6 | async-start | bytes 131072 | tf_op jit(solution)/shard_map/all_to_all | solution.py:90
  458.4 7.4 %all-to-all-done.6 = f32[32,1,512]{2,1,0:T(1,128)S(1)} async-done(((f32[32,1,512]{2,1,0:T(1,128)}), f32[32,1,512]{2,1,0:T(1,128)S(1)}, u32[]{:S(2)}, u32[]{:S(2)}) %all-to-all-start.6) | async-done | bytes 65568 | tf_op jit(solution)/shard_map/all_to_all | solution.py:90
  466.5 1.9 broadcast_select_fusion
  468.7 1.0 convolution_subtract_fusion
  469.8 1.0 convolution_bitcast_fusion
  470.8 2.2 fusion.2
  (43 shorter events, 6.3 us)
Async XLA Ops:
  0.6 448.1 %copy-start = (f32[512,512]{1,0:T(8,128)S(1)}, f32[512,512]{1,0:T(8,128)}, u32[]{:S(2)}) copy-start(f32[512,512]{1,0:T(8,128)} %param.12) | copy-start | bytes 3145732
  10.8 240.8 %all-to-all-start = ((f32[32,128,1024]{2,1,0:T(8,128)}), f32[32,128,1024]{2,1,0:T(8,128)}, u32[]{:S(2)}, u32[]{:S(2)}) async-start(f32[32,128,1024]{2,1,0:T(8,128)} %stack.2), calls=%async_computation | async-start | bytes 33554432 | tf_op jit(solution)/shard_map/all_to_all | solution.py:16
  253.2 23.4 %all-to-all-start.2 = ((f32[4,128,1024]{2,1,0:T(8,128)}), f32[4,128,1024]{2,1,0:T(8,128)S(1)}, u32[]{:S(2)}, u32[]{:S(2)}) async-start(f32[4,128,1024]{2,1,0:T(8,128)} %broadcast_in_dim.7), calls=%async_computation.2 | async-start | bytes 4194304 | tf_op jit(solution)/shard_map/all_to_all | solution.py:45
  283.7 1.6 copy-start.1
  285.5 13.6 %collective-permute-start = (f32[768,512]{1,0:T(8,128)S(1)}, f32[768,512]{1,0:T(8,128)}, u32[]{:S(2)}, u32[]{:S(2)}) collective-permute-start(f32[768,512]{1,0:T(8,128)S(1)} %dynamic-slice_bitcast_fusion), channel_id=1, source_target_pairs={{0,1},{1,0},{2,3},{3,2},{4,5},{5,4},{6,7},{7,6},{8,9},{9,8},{10,11... | collective-permute-start | bytes 4718600 | tf_op jit(solution)/shard_map/ppermute | solution.py:40
  302.8 42.9 %copy-start.8 = (f32[1,1,512]{2,1,0:T(1,128)S(1)}, f32[1,1,512]{2,1,0:T(1,128)}, u32[]{:S(2)}) copy-start(f32[1,1,512]{2,1,0:T(1,128)} %param.15) | copy-start | bytes 6148
  302.8 70.0 %all-to-all-start.3 = ((f32[64,12,512]{2,1,0:T(8,128)}), f32[64,12,512]{2,1,0:T(8,128)S(1)}, u32[]{:S(2)}, u32[]{:S(2)}) async-start(f32[64,12,512]{2,1,0:T(8,128)} %reshape.58), calls=%async_computation.3 | async-start | bytes 4194304 | tf_op jit(solution)/shard_map/all_to_all | solution.py:56
  372.8 13.5 %all-to-all-start.5 = ((f32[32,1,16]{2,1,0:T(1,128)}), f32[32,1,16]{2,1,0:T(1,128)S(1)}, u32[]{:S(2)}, u32[]{:S(2)}) async-start(f32[32,1,16]{2,1,0:T(1,128)} %bitcast.14), calls=%async_computation.5 | async-start | bytes 32768 | tf_op jit(solution)/shard_map/all_to_all | solution.py:72
  418.9 28.0 %all-to-all-start.1 = ((f32[4,128,1024]{2,1,0:T(8,128)}), f32[4,128,1024]{2,1,0:T(8,128)}, u32[]{:S(2)}, u32[]{:S(2)}) async-start(f32[4,128,1024]{2,1,0:T(8,128)} %bitcast.4), calls=%async_computation.1 | async-start | bytes 4194304 | tf_op jit(solution)/shard_map/all_to_all | solution.py:85
  423.3 4.2 copy-start.9
  423.3 4.2 copy-start.10
  424.7 41.8 %collective-permute-start.1 = (f32[768,512]{1,0:T(8,128)}, f32[768,512]{1,0:T(8,128)}, u32[]{:S(2)}, u32[]{:S(2)}) collective-permute-start(f32[768,512]{1,0:T(8,128)} %reshape.59), channel_id=1, source_target_pairs={{0,1},{1,0},{2,3},{3,2},{4,5},{5,4},{6,7},{7,6},{8,9},{9,8},{10,11... | collective-permute-start | bytes 4718600 | tf_op jit(solution)/shard_map/ppermute | solution.py:40
  448.7 17.8 %copy-start.2 = (f32[768,512]{1,0:T(8,128)S(1)}, f32[768,512]{1,0:T(8,128)}, u32[]{:S(2)}) copy-start(f32[768,512]{1,0:T(8,128)} %reshape.59) | copy-start | bytes 4718596
  448.7 19.7 %copy-start.6 = (f32[128,512]{1,0:T(8,128)}, f32[128,512]{1,0:T(8,128)S(1)}, u32[]{:S(2)}) copy-start(f32[128,512]{1,0:T(8,128)S(1)} %slice_negate_fusion) | copy-start | bytes 786436
  449.2 0.7 copy-start.7
  450.8 15.0 %all-to-all-start.6 = ((f32[32,1,512]{2,1,0:T(1,128)}), f32[32,1,512]{2,1,0:T(1,128)S(1)}, u32[]{:S(2)}, u32[]{:S(2)}) async-start(f32[32,1,512]{2,1,0:T(1,128)} %copy.21), calls=%async_computation.6 | async-start | bytes 131072 | tf_op jit(solution)/shard_map/all_to_all | solution.py:90
  466.5 2.1 copy-start.5
  468.7 1.0 copy-start.3
  469.8 3.2 copy-start.4
